TPU v7x, 256 devices: a whole 4x4x8 slice. The times are simulated.
256 devices in a mesh: row: 16 (over z_hi, y, core), col: 16 (over z_lo, x).
Axes of the slice: x: 4, y: 4, z: 8 (z_hi: 2, z_lo: 4; z = z_hi * 4 + z_lo), core: 2. Of those that a mesh axis runs over, the one named last changes fastest.
Arguments:
- features: float32 [131072, 256], P(('row', 'col')), may hold values from -6 to 6
- self_weight: float32 [256, 128], replicated, may hold values from -0.375 to 0.375
- neigh_weight: float32 [256, 128], replicated, may hold values from -0.75 to 0.75
- out_bias: float32 [128], replicated, may hold values from -3 to 3
- adjacency_tiles: int32 [1024, 32, 128, 128], P('row', 'col'), may hold values from 0 to 3, as said below
- tile_columns: int32 [1024, 32], P('row', 'col'), may hold values from 0 to 63
- live_counts: int32 [1024, 16], P('row', 'col'), may hold values from 1 to 2, as said below
- cotangent: float32 [131072, 128], P(('row', 'col')), may hold values from -6 to 6
Outputs:
- hidden_out: float32 [131072, 128], P(('row', 'col'))
- grad_features: float32 [131072, 256], P(('row', 'col'))
- grad_self: float32 [256, 128], replicated
- grad_neigh: float32 [256, 128], replicated
- grad_bias: float32 [128], replicated
Inputs may be any that keep to these rules, and one draw needn't show every extreme that they name: `adjacency_tiles`: edge multiplicities; most entries are zero. `live_counts`: slots at or after this count in a tile-row's block are ignored, whatever they hold.
All inputs are finite; a program needn't handle non-finite values.
Results may differ from a plain program's by a relative error of at most 0.0003.
Values sent between devices are 32-bit elements; how exact they have to be, the bound alone decides.
A program may use at most 128 MiB of HBM per device.

v0:
```python
import math
import jax
import jax.numpy as jnp
from jax import lax
from jax.sharding import PartitionSpec as P


def live_weights(tile_values, count_block):
    slot_ids = jnp.arange(tile_values.shape[1], dtype=jnp.int32)
    live_slots = (slot_ids[None, :] < count_block).astype(jnp.float32)
    return tile_values.astype(jnp.float32) * live_slots[:, :, None, None]


def forward_tiles(weighted, column_block, source):
    tile_size = weighted.shape[2]
    feature_width = source.shape[1]
    source_tiles = source.reshape(-1, tile_size, feature_width)
    picked = source_tiles[column_block]
    products = jnp.einsum("tkab,tkbw->taw", weighted, picked, precision=lax.Precision.HIGHEST)
    return products.reshape(-1, feature_width)


def backward_tiles(weighted, column_block, source, col_tiles):
    tile_size = weighted.shape[2]
    feature_width = source.shape[1]
    source_tiles = source.reshape(-1, tile_size, feature_width)
    spread = jnp.einsum("tkab,taw->tkbw", weighted, source_tiles, precision=lax.Precision.HIGHEST)
    merged = jax.ops.segment_sum(
        spread.reshape(-1, tile_size, feature_width),
        column_block.reshape(-1),
        num_segments=col_tiles,
    )
    return merged.reshape(-1, feature_width)


def local(
    features,
    self_weight,
    neigh_weight,
    out_bias,
    adjacency_tiles,
    tile_columns,
    live_counts,
    cotangent,
):
    highest = lax.Precision.HIGHEST
    weighted = live_weights(adjacency_tiles, live_counts)
    degree_part = jnp.sum(weighted, axis=(1, 3)).reshape(-1)
    local_self = jnp.dot(features, self_weight, precision=highest)
    gathered = lax.all_gather(features, "row", axis=0, tiled=True)
    partial_rows = forward_tiles(weighted, tile_columns, gathered)
    summed, degree_sum = (
        lax.psum_scatter(partial_rows, "col", scatter_dimension=0, tiled=True),
        lax.psum_scatter(degree_part, "col", scatter_dimension=0, tiled=True),
    )
    degree = 1.0 + degree_sum
    aggregated = summed / degree[:, None]
    pre_act = local_self + jnp.dot(aggregated, neigh_weight, precision=highest) + out_bias
    hidden_out = jax.nn.silu(pre_act)
    sig_value = jax.nn.sigmoid(pre_act)
    grad_pre = cotangent * sig_value * (1.0 + pre_act * (1.0 - sig_value))
    scaled = grad_pre / degree[:, None]
    block_rows = lax.all_gather(scaled, "col", axis=0, tiled=True)
    col_tiles = features.shape[0] * lax.axis_size("row") // adjacency_tiles.shape[2]
    back_part = backward_tiles(weighted, tile_columns, block_rows, col_tiles)
    back_rows = lax.psum_scatter(back_part, "row", scatter_dimension=0, tiled=True)
    grad_features = jnp.dot(grad_pre, self_weight.T, precision=highest) + jnp.dot(
        back_rows, neigh_weight.T, precision=highest
    )
    grad_self_part = jnp.dot(features.T, grad_pre, precision=highest)
    grad_neigh_part = jnp.dot(aggregated.T, grad_pre, precision=highest)
    grad_bias_part = jnp.sum(grad_pre, axis=0)
    totals = lax.psum((grad_self_part, grad_neigh_part, grad_bias_part), ("row", "col"))
    node_total = features.shape[0] * lax.axis_size("row") * lax.axis_size("col")
    factor = 1.0 / math.sqrt(node_total)
    return (hidden_out, grad_features, totals[0] * factor, totals[1] * factor, totals[2] * factor)


def solution(mesh):
    return jax.shard_map(
        local,
        mesh=mesh,
        in_specs=(
            P(("row", "col"), None),
            P(),
            P(),
            P(),
            P("row", "col", None, None),
            P("row", "col"),
            P("row", "col"),
            P(("row", "col"), None),
        ),
        out_specs=(P(("row", "col"), None), P(("row", "col"), None), P(), P(), P()),
        check_vma=False,
    )
```

profile of v0, /device:TPU:2, one launch (start us, length us, event | category | flops | bytes accessed | tf_op | source)
XLA Modules:
  0.0 724.2 jit_solution(1517068199887440945)
XLA Ops:
  7.2 0.0 copy-start
  7.2 0.0 all-gather.3.cloned.1.call-start
  7.2 0.7 all-gather.3.cloned.1.call-update
  7.9 0.0 reduce-scatter.3.cloned.1.call-start
  8.0 0.7 compare_select_fusion
  8.6 0.1 copy.25
  8.7 0.1 reshape.61
  8.9 0.7 fusion.8
  9.6 112.4 %all-gather.3.cloned.1.call-done = f32[8192,256]{1,0:T(8,128)} async-done(((f32[512,256]{1,0:T(8,128)}), f32[8192,256]{1,0:T(8,128)}) %all-gather.3.cloned.1.call-update) | async-done | bytes 8388624 | tf_op jit(solution)/shard_map/all_gather | solution.py:50
  122.0 13.2 %gather_fusion = f32[128,128,256]{2,1,0:T(8,128)} fusion(f32[64,128,256]{2,1,0:T(8,128)} %bitcast.33, s32[1024]{0:T(1024)S(1)} %pad_clamp_fusion), kind=kCustom, calls=%fused_computation | custom fusion | bytes 33554944 | tf_op jit(solution)/shard_map/gather | solution.py:18
  135.3 22.8 %fusion.2 = f32[64,128,256,1]{2,1,3,0:T(8,128)} fusion(f32[64,2,128,256]{3,2,1,0:T(8,128)} %bitcast.30, s32[64,2,128,128]{3,2,1,0:T(8,128)} %param.12, f32[64,2]{1,0:T(8,128)S(1)} %fusion.8), kind=kOutput, calls=%fused_computation.5 | convolution fusion | flops 6446645248 | bytes 33554944 | tf_op jit(solution)/shard_map/tkab,tkbw->taw/dot_general | solution.py:19
  158.1 0.0 copy-start.4
  158.1 0.0 copy-start.5
  158.1 0.0 reduce-scatter.3.cloned.1.call-update
  158.2 0.0 copy-start.3
  158.2 0.0 all-gather.5.cloned.1.call-start
  158.2 0.6 copy-done.6
  158.8 0.6 dynamic-slice
  160.0 5.1 fusion.1
  165.1 71.6 %all-reduce = f32[8192]{0:T(1024)S(1)} all-reduce(f32[8192]{0:T(1024)S(1)} %bitcast.36), channel_id=3, replica_groups=mesh['row'=16,'col'=16] {'col'}, use_global_device_ids=true, to_apply=%region_2.0.clone | all-reduce | flops 8192 | bytes 65536
  236.6 0.1 dynamic-slice_add_fusion
  236.7 0.6 fusion.10
  237.3 21.3 %reduce-scatter.3.cloned.1.call-done = f32[512,256]{1,0:T(8,128)} async-done(((f32[8192,256]{1,0:T(8,128)}), f32[512,256]{1,0:T(8,128)}) %reduce-scatter.3.cloned.1.call-update) | async-done | bytes 524304 | tf_op jit(solution)/shard_map/reduce_scatter | solution.py:53
  258.6 0.0 copy-done.5
  258.6 2.4 fusion.9
  261.0 0.8 broadcast_divide_fusion.1
  261.8 0.0 all-gather.5.cloned.1.call-update
  261.9 0.2 all-reduce.4.cloned.1.call-start
  262.1 0.1 copy.26
  262.2 0.1 reshape.69
  262.3 1.3 convolution_bitcast_fusion
  263.6 2.4 fusion.7
  266.0 0.0 all-reduce.4.cloned.1.call-update
  266.0 0.0 reduce-scatter.5.cloned.1.call-start
  266.1 82.5 %all-gather.5.cloned.1.call-done = f32[8192,128]{1,0:T(8,128)} async-done(((f32[512,128]{1,0:T(8,128)}), f32[8192,128]{1,0:T(8,128)}) %all-gather.5.cloned.1.call-update) | async-done | bytes 4194320 | tf_op jit(solution)/shard_map/all_gather | solution.py:63
  348.6 19.8 %fusion = f32[64,2,128,128]{3,2,1,0:T(8,128)} fusion(f32[64,128,128,1]{2,1,3,0:T(8,128)} %bitcast.35, s32[64,2,128,128]{3,2,1,0:T(8,128)} %param.12, f32[64,2]{1,0:T(8,128)S(1)} %fusion.8), kind=kOutput, calls=%fused_computation.3 | convolution fusion | flops 3225419776 | bytes 20972032 | tf_op jit(solution)/shard_map/tkab,taw->tkbw/dot_general | solution.py:27
  368.4 2.5 broadcast_in_dim.5
  370.8 26.9 %scatter_fusion = f32[64,128,128]{2,1,0:T(8,128)} fusion(f32[64,128,128]{2,1,0:T(8,128)} %broadcast_in_dim.5, s32[128]{0:T(128)S(1)} %reshape.69, f32[128,128,128]{2,1,0:T(8,128)} %bitcast.34), kind=kCustom, calls=%fused_computation.1 | custom fusion | flops 2097152 | bytes 25166336 | tf_op jit(solution)/shard_map/scatter-add | solution.py:28
  397.7 0.0 reduce-scatter.5.cloned.1.call-update
  397.8 75.4 %psum.23 = f32[128]{0:T(128)S(1)} all-reduce(f32[128]{0:T(128)S(1)} %get-tuple-element.22), channel_id=1, replica_groups=mesh['row'=16,'col'=16] {'row','col'}, use_global_device_ids=true, to_apply=%region_8.9 | all-reduce | flops 128 | bytes 1024 | tf_op jit(solution)/shard_map/psum | solution.py:73
  473.1 0.5 broadcast_multiply_fusion.2
  473.7 0.6 fusion.11
  474.2 133.8 %all-reduce.4.cloned.1.call-done = (f32[256,128]{0,1:T(8,128)}, f32[256,128]{0,1:T(8,128)}) async-done(((f32[256,128]{0,1:T(8,128)}, f32[256,128]{0,1:T(8,128)}), (f32[256,128]{0,1:T(8,128)}, f32[256,128]{0,1:T(8,128)})) %all-reduce.4.cloned.1.call-update) | async-done | bytes 262160 | tf_op jit(solution)/shard_map/psum | solution.py:73
  608.1 1.0 broadcast_multiply_fusion
  609.1 0.8 copy.29
  609.8 0.8 copy.30
  610.6 104.8 %reduce-scatter.5.cloned.1.call-done = f32[512,128]{1,0:T(8,128)} async-done(((f32[8192,128]{1,0:T(8,128)}), f32[512,128]{1,0:T(8,128)}) %reduce-scatter.5.cloned.1.call-update) | async-done | bytes 262160 | tf_op jit(solution)/shard_map/reduce_scatter | solution.py:66
  715.4 2.3 convolution_add_fusion
  (9 shorter events, 0.0 us)
Async XLA Ops:
  7.2 251.4 %copy-start = (f32[256,128]{1,0:T(8,128)S(1)}, f32[256,128]{1,0:T(8,128)}, u32[]{:S(2)}) copy-start(f32[256,128]{1,0:T(8,128)} %param.10) | copy-start | bytes 393220
  7.2 114.9 %all-gather.3.cloned.1.call-start = ((), (), s32[]{:S(2)}) async-start(), calls=%async_computation.2 | async-start | bytes 8912896 | tf_op jit(solution)/shard_map/all_gather | solution.py:50
  7.9 250.7 %reduce-scatter.3.cloned.1.call-start = ((), (), s32[]{:S(2)}) async-start(), calls=%async_computation.3 | async-start | bytes 8912896 | tf_op jit(solution)/shard_map/reduce_scatter | solution.py:53
  158.1 0.7 copy-start.6
  158.1 78.6 %copy-start.1 = (f32[512,256]{1,0:T(8,128)S(1)}, f32[512,256]{1,0:T(8,128)}, u32[]{:S(2)}) copy-start(f32[512,256]{1,0:T(8,128)} %param.8) | copy-start | bytes 1572868
  158.1 78.6 %copy-start.2 = (f32[256,128]{1,0:T(8,128)S(1)}, f32[256,128]{1,0:T(8,128)}, u32[]{:S(2)}) copy-start(f32[256,128]{1,0:T(8,128)} %param.9) | copy-start | bytes 393220
  158.1 100.5 %copy-start.4 = (f32[512,128]{1,0:T(8,128)S(1)}, f32[512,128]{1,0:T(8,128)}, u32[]{:S(2)}) copy-start(f32[512,128]{1,0:T(8,128)} %param.15) | copy-start | bytes 786436
  158.1 100.5 %copy-start.5 = (f32[128]{0:T(128)S(1)}, f32[128]{0:T(128)}, u32[]{:S(2)}) copy-start(f32[128]{0:T(128)} %param.11) | copy-start | bytes 1540
  158.2 103.9 %copy-start.3 = (s32[64,2]{0,1:T(2,128)S(1)}, s32[64,2]{0,1:T(2,128)}, u32[]{:S(2)}) copy-start(s32[64,2]{0,1:T(2,128)} %param.13) | copy-start | bytes 1540
  158.2 190.4 %all-gather.5.cloned.1.call-start = ((), (), s32[]{:S(2)}) async-start(), calls=%async_computation.4 | async-start | bytes 4456448 | tf_op jit(solution)/shard_map/all_gather | solution.py:63
  261.9 346.2 %all-reduce.4.cloned.1.call-start = ((), (), s32[]{:S(2)}) async-start(), calls=%async_computation.6 | async-start | bytes 524288 | tf_op jit(solution)/shard_map/psum | solution.py:73
  266.0 449.3 %reduce-scatter.5.cloned.1.call-start = ((), (), s32[]{:S(2)}) async-start(), calls=%async_computation.5 | async-start | bytes 4456448 | tf_op jit(solution)/shard_map/reduce_scatter | solution.py:66
Sparse Core Ops, SparseCore 0:
  10.7 111.2 all-gather.2
  158.3 100.2 reduce-scatter.2
  262.0 86.5 all-gather.4
  354.6 253.3 all-reduce.3
  612.2 103.0 reduce-scatter.4
where the time goes:
time: 725 us; the launch traced here: 724 us
  waiting for transfers between devices  456 us (63%)
  blocking collectives  147 us (20%)
  matrix products  52.1 us (7%)
  other arithmetic  35.8 us (5%)
  local copies, waits for them, and re-layouts  18.9 us (3%)
  between operations  14.5 us (2%)
    psum x1, waiting for transfers between devices, local(): lax.psum((grad_self_part, grad_neigh_part, grad_bias_part), ('row', 'col'))  134 us
    all_gather x1, waiting for transfers between devices, local(): gathered = lax.all_gather(features, 'row', axis=0, tiled=True)  112 us
    reduce_scatter x1, waiting for transfers between devices, local(): lax.psum_scatter(back_part, 'row', scatter_dimension=0, tiled=True)  105 us
    all_gather x1, waiting for transfers between devices, local(): block_rows = lax.all_gather(scaled, 'col', axis=0, tiled=True)  82.5 us
    psum x1, blocking collectives, local(): lax.psum((grad_self_part, grad_neigh_part, grad_bias_part), ('row', 'col'))  75.4 us
    unnamed x1, blocking collectives  71.6 us
    scatter-add x1, other arithmetic, backward_tiles(): jax.ops.segment_sum(spread.reshape(-1, tile_size, feature_width), column_...  26.9 us
    dot_general x1, matrix products, forward_tiles(): jnp.einsum('tkab,tkbw->taw', weighted, picked, precision=lax.Precision.HI...  22.8 us
  transfers between devices with their start and end apart: 5, of which 5 were waited for; matrix products, arithmetic and copies ran while one was open for 9% of the time, Pallas kernels for 0%

commit v1 on v0

--- a/solution.py
+++ b/solution.py
@@ -60,7 +60,9 @@
     sig_value = jax.nn.sigmoid(pre_act)
     grad_pre = cotangent * sig_value * (1.0 + pre_act * (1.0 - sig_value))
     scaled = grad_pre / degree[:, None]
-    block_rows = lax.all_gather(scaled, "col", axis=0, tiled=True)
+    block_rows = jnp.concatenate(
+        lax.all_to_all(jnp.stack([scaled] * lax.axis_size("col")), "col", 0, 0), axis=0
+    )
     col_tiles = features.shape[0] * lax.axis_size("row") // adjacency_tiles.shape[2]
     back_part = backward_tiles(weighted, tile_columns, block_rows, col_tiles)
     back_rows = lax.psum_scatter(back_part, "row", scatter_dimension=0, tiled=True)

time: 725 us -> 665 us (0.917)
  waiting for transfers between devices: 456 us -> 373 us
  blocking collectives: 147 us -> 161 us
  starting transfers between devices: 0.38 us -> 7.74 us
    all_gather x1 -> x0, waiting for transfers between devices: 82.5 us -> none  [local(): block_rows = lax.all_gather(scaled, 'col', axis=0, tiled=True)]
    all_to_all x0 -> x1, waiting for transfers between devices: none -> 69 us  [local(): lax.all_to_all(jnp.stack([scaled] * lax.axis_size('col')), 'col', 0, 0)]
    psum x1, waiting for transfers between devices: 134 us -> 65.1 us  [local(): lax.psum((grad_self_part, grad_neigh_part, grad_bias_part), ('row', 'col'))]
    psum x1, blocking collectives: 75.4 us -> 89.6 us  [local(): lax.psum((grad_self_part, grad_neigh_part, grad_bias_part), ('row', 'col'))]
    all_to_all x0 -> x1, starting transfers between devices: none -> 7.41 us  [local(): lax.all_to_all(jnp.stack([scaled] * lax.axis_size('col')), 'col', 0, 0)]
  transfers between devices with their start and end apart: 5 -> 5, of which waited for: 5 -> 5; matrix products, arithmetic and copies ran while one was open for 9% -> 10% of each run, Pallas kernels for 0% -> 0%
where the time goes in v1:
time: 665 us; the launch traced here: 664 us
  waiting for transfers between devices  373 us (56%)
  blocking collectives  161 us (24%)
  matrix products  51.2 us (8%)
  other arithmetic  35.1 us (5%)
  local copies, waits for them, and re-layouts  21.3 us (3%)
  between operations  14.5 us (2%)
  starting transfers between devices  7.74 us (1%)
    all_gather x1, waiting for transfers between devices, local(): gathered = lax.all_gather(features, 'row', axis=0, tiled=True)  112 us
    reduce_scatter x1, waiting for transfers between devices, local(): lax.psum_scatter(back_part, 'row', scatter_dimension=0, tiled=True)  105 us
    psum x1, blocking collectives, local(): lax.psum((grad_self_part, grad_neigh_part, grad_bias_part), ('row', 'col'))  89.6 us
    unnamed x1, blocking collectives  71.6 us
    all_to_all x1, waiting for transfers between devices, local(): lax.all_to_all(jnp.stack([scaled] * lax.axis_size('col')), 'col', 0, 0)  69 us
    psum x1, waiting for transfers between devices, local(): lax.psum((grad_self_part, grad_neigh_part, grad_bias_part), ('row', 'col'))  65.1 us
    scatter-add x1, other arithmetic, backward_tiles(): jax.ops.segment_sum(spread.reshape(-1, tile_size, feature_width), column_...  26.9 us
    dot_general x1, matrix products, forward_tiles(): jnp.einsum('tkab,tkbw->taw', weighted, picked, precision=lax.Precision.HI...  22.8 us
  transfers between devices with their start and end apart: 5, of which 5 were waited for; matrix products, arithmetic and copies ran while one was open for 10% of the time, Pallas kernels for 0%

profile of v1, /device:TPU:2, one launch (start us, length us, event | category | flops | bytes accessed | tf_op | source)
XLA Modules:
  0.0 664.1 jit_solution(15552702959407788897)
XLA Ops:
  7.2 0.0 copy-start
  7.2 0.0 all-gather.2.cloned.1.call-start
  7.2 0.7 all-gather.2.cloned.1.call-update
  7.9 0.0 reduce-scatter.3.cloned.1.call-start
  8.0 0.7 compare_select_fusion
  8.6 0.1 copy.25
  8.7 0.1 reshape.59
  8.9 0.7 fusion.8
  9.6 112.4 %all-gather.2.cloned.1.call-done = f32[8192,256]{1,0:T(8,128)} async-done(((f32[512,256]{1,0:T(8,128)}), f32[8192,256]{1,0:T(8,128)}) %all-gather.2.cloned.1.call-update) | async-done | bytes 8388624 | tf_op jit(solution)/shard_map/all_gather | solution.py:50
  122.0 13.2 %gather_fusion = f32[128,128,256]{2,1,0:T(8,128)} fusion(f32[64,128,256]{2,1,0:T(8,128)} %bitcast.33, s32[1024]{0:T(1024)S(1)} %pad_clamp_fusion), kind=kCustom, calls=%fused_computation | custom fusion | bytes 33554944 | tf_op jit(solution)/shard_map/gather | solution.py:18
  135.3 22.8 %fusion.2 = f32[64,128,256,1]{2,1,3,0:T(8,128)} fusion(f32[64,2,128,256]{3,2,1,0:T(8,128)} %bitcast.30, s32[64,2,128,128]{3,2,1,0:T(8,128)} %param.12, f32[64,2]{1,0:T(8,128)S(1)} %fusion.8), kind=kOutput, calls=%fused_computation.5 | convolution fusion | flops 6446645248 | bytes 33554944 | tf_op jit(solution)/shard_map/tkab,tkbw->taw/dot_general | solution.py:19
  158.1 0.0 copy-start.5
  158.1 0.0 copy-start.6
  158.1 0.0 reduce-scatter.3.cloned.1.call-update
  158.2 0.6 copy-done.7
  158.8 0.6 dynamic-slice
  160.0 5.1 fusion.1
  165.1 71.6 %all-reduce = f32[8192]{0:T(1024)S(1)} all-reduce(f32[8192]{0:T(1024)S(1)} %bitcast.35), channel_id=3, replica_groups=mesh['row'=16,'col'=16] {'col'}, use_global_device_ids=true, to_apply=%region_2.0.clone | all-reduce | flops 8192 | bytes 65536
  236.6 0.1 dynamic-slice_add_fusion
  236.7 0.6 fusion.10
  237.3 0.0 copy-start.3
  237.3 21.3 %reduce-scatter.3.cloned.1.call-done = f32[512,256]{1,0:T(8,128)} async-done(((f32[8192,256]{1,0:T(8,128)}), f32[512,256]{1,0:T(8,128)}) %reduce-scatter.3.cloned.1.call-update) | async-done | bytes 524304 | tf_op jit(solution)/shard_map/reduce_scatter | solution.py:53
  258.6 0.0 copy-done.6
  258.6 2.5 fusion.9
  261.1 0.1 broadcast_divide_fusion.1
  261.2 2.3 stack.2
  263.6 7.4 %all-to-all-start = ((f32[16,512,128]{2,1,0:T(8,128)}), f32[16,512,128]{2,1,0:T(8,128)}, u32[]{:S(2)}, u32[]{:S(2)}) async-start(f32[16,512,128]{2,1,0:T(8,128)} %stack.2), calls=%async_computation.1 | async-start | bytes 8388608 | tf_op jit(solution)/shard_map/all_to_all | solution.py:64
  271.0 0.2 all-reduce.4.cloned.1.call-start
  271.2 0.1 copy.26
  271.3 0.1 reshape.67
  271.4 1.3 convolution_bitcast_fusion
  272.7 1.4 fusion.7
  274.1 0.0 all-reduce.4.cloned.1.call-update
  274.1 0.0 reduce-scatter.5.cloned.1.call-start
  274.1 69.0 %all-to-all-done = f32[16,512,128]{2,1,0:T(8,128)} async-done(((f32[16,512,128]{2,1,0:T(8,128)}), f32[16,512,128]{2,1,0:T(8,128)}, u32[]{:S(2)}, u32[]{:S(2)}) %all-to-all-start) | async-done | bytes 4194336 | tf_op jit(solution)/shard_map/all_to_all | solution.py:64
  343.1 19.8 %fusion = f32[64,2,128,128]{3,2,1,0:T(8,128)} fusion(f32[64,128,128,1]{2,1,3,0:T(8,128)} %bitcast.9, s32[64,2,128,128]{3,2,1,0:T(8,128)} %param.12, f32[64,2]{1,0:T(8,128)S(1)} %fusion.8), kind=kOutput, calls=%fused_computation.3 | convolution fusion | flops 3225419776 | bytes 20972032 | tf_op jit(solution)/shard_map/tkab,taw->tkbw/dot_general | solution.py:27
  362.9 2.5 broadcast_in_dim.5
  365.4 26.9 %scatter_fusion = f32[64,128,128]{2,1,0:T(8,128)} fusion(f32[64,128,128]{2,1,0:T(8,128)} %broadcast_in_dim.5, s32[128]{0:T(128)S(1)} %reshape.67, f32[128,128,128]{2,1,0:T(8,128)} %bitcast.34), kind=kCustom, calls=%fused_computation.1 | custom fusion | flops 2097152 | bytes 25166336 | tf_op jit(solution)/shard_map/scatter-add | solution.py:28
  392.2 0.0 reduce-scatter.5.cloned.1.call-update
  392.2 89.6 %psum.23 = f32[128]{0:T(128)S(1)} all-reduce(f32[128]{0:T(128)S(1)} %get-tuple-element.22), channel_id=1, replica_groups=mesh['row'=16,'col'=16] {'row','col'}, use_global_device_ids=true, to_apply=%region_8.9 | all-reduce | flops 128 | bytes 1024 | tf_op jit(solution)/shard_map/psum | solution.py:75
  481.8 0.5 broadcast_multiply_fusion.2
  482.3 0.6 fusion.11
  482.9 65.1 %all-reduce.4.cloned.1.call-done = (f32[256,128]{0,1:T(8,128)}, f32[256,128]{0,1:T(8,128)}) async-done(((f32[256,128]{0,1:T(8,128)}, f32[256,128]{0,1:T(8,128)}), (f32[256,128]{0,1:T(8,128)}, f32[256,128]{0,1:T(8,128)})) %all-reduce.4.cloned.1.call-update) | async-done | bytes 262160 | tf_op jit(solution)/shard_map/psum | solution.py:75
  548.0 1.0 broadcast_multiply_fusion
  549.0 0.8 copy.29
  549.7 0.8 copy.30
  550.5 104.8 %reduce-scatter.5.cloned.1.call-done = f32[512,128]{1,0:T(8,128)} async-done(((f32[8192,128]{1,0:T(8,128)}), f32[512,128]{1,0:T(8,128)}) %reduce-scatter.5.cloned.1.call-update) | async-done | bytes 262160 | tf_op jit(solution)/shard_map/reduce_scatter | solution.py:68
  655.3 2.3 convolution_add_fusion
  (11 shorter events, 0.0 us)
Async XLA Ops:
  7.2 251.4 %copy-start = (f32[256,128]{1,0:T(8,128)S(1)}, f32[256,128]{1,0:T(8,128)}, u32[]{:S(2)}) copy-start(f32[256,128]{1,0:T(8,128)} %param.10) | copy-start | bytes 393220
  7.2 114.9 %all-gather.2.cloned.1.call-start = ((), (), s32[]{:S(2)}) async-start(), calls=%async_computation.3 | async-start | bytes 8912896 | tf_op jit(solution)/shard_map/all_gather | solution.py:50
  7.9 250.7 %reduce-scatter.3.cloned.1.call-start = ((), (), s32[]{:S(2)}) async-start(), calls=%async_computation.4 | async-start | bytes 8912896 | tf_op jit(solution)/shard_map/reduce_scatter | solution.py:53
  158.1 0.7 copy-start.7
  158.1 78.6 %copy-start.1 = (f32[512,256]{1,0:T(8,128)S(1)}, f32[512,256]{1,0:T(8,128)}, u32[]{:S(2)}) copy-start(f32[512,256]{1,0:T(8,128)} %param.8) | copy-start | bytes 1572868
  158.1 78.6 %copy-start.2 = (f32[256,128]{1,0:T(8,128)S(1)}, f32[256,128]{1,0:T(8,128)}, u32[]{:S(2)}) copy-start(f32[256,128]{1,0:T(8,128)} %param.9) | copy-start | bytes 393220
  158.1 100.5 %copy-start.5 = (f32[512,128]{1,0:T(8,128)S(1)}, f32[512,128]{1,0:T(8,128)}, u32[]{:S(2)}) copy-start(f32[512,128]{1,0:T(8,128)} %param.15) | copy-start | bytes 786436
  158.1 100.5 %copy-start.6 = (f32[128]{0:T(128)S(1)}, f32[128]{0:T(128)}, u32[]{:S(2)}) copy-start(f32[128]{0:T(128)} %param.11) | copy-start | bytes 1540
  237.3 33.9 %copy-start.3 = (s32[64,2]{0,1:T(2,128)S(1)}, s32[64,2]{0,1:T(2,128)}, u32[]{:S(2)}) copy-start(s32[64,2]{0,1:T(2,128)} %param.13) | copy-start | bytes 1540
  258.6 14.1 %copy-start.4 = (f32[512,256]{1,0:T(8,128)S(1)}, f32[512,256]{1,0:T(8,128)}, u32[]{:S(2)}) copy-start(f32[512,256]{1,0:T(8,128)} %reduce-scatter.3.cloned.1.call-done) | copy-start | bytes 1572868
  263.6 79.6 %all-to-all-start = ((f32[16,512,128]{2,1,0:T(8,128)}), f32[16,512,128]{2,1,0:T(8,128)}, u32[]{:S(2)}, u32[]{:S(2)}) async-start(f32[16,512,128]{2,1,0:T(8,128)} %stack.2), calls=%async_computation.1 | async-start | bytes 8388608 | tf_op jit(solution)/shard_map/all_to_all | solution.py:64
  271.0 277.0 %all-reduce.4.cloned.1.call-start = ((), (), s32[]{:S(2)}) async-start(), calls=%async_computation.6 | async-start | bytes 524288 | tf_op jit(solution)/shard_map/psum | solution.py:75
  274.1 381.2 %reduce-scatter.5.cloned.1.call-start = ((), (), s32[]{:S(2)}) async-start(), calls=%async_computation.5 | async-start | bytes 4456448 | tf_op jit(solution)/shard_map/reduce_scatter | solution.py:68
Sparse Core Ops, SparseCore 0:
  10.7 111.2 all-gather.1
  158.3 100.2 reduce-scatter.2
  277.9 270.0 all-reduce.3
  552.2 103.0 reduce-scatter.4
